TPU v7x, 32 devices: a whole 2x2x4 slice. The times are simulated.
32 devices in a mesh: seg: 8 (over z, y), ctl: 4 (over x, core).
Axes of the slice: x: 2, y: 2, z: 4, core: 2. Of those that a mesh axis runs over, the one named last changes fastest.
Arguments:
- transition: float32 [8, 1024, 1024], P('seg'), may hold values from -1 to 1
- control_map: float32 [8, 1024, 256], P('seg'), may hold values from -1.5 to 1.5
- weights: float32 [8, 1024], P('seg'), may hold values from 0.01 to 0.5
Outputs:
- sensitivity: float32 [8, 1024, 2048], P('seg', None, 'ctl')
- hessian_tiles: float32 [4, 512, 512], P('ctl', 'seg')
All inputs are finite; a program needn't handle non-finite values.
Results may differ from a plain program's by a relative error of at most 0.0003.
Values sent between devices are 32-bit elements; how exact they have to be, the bound alone decides.
No kernel may reach another device: no remote copies, remote signals or barrier semaphores. Data moves between devices by JAX's collectives and lax.ppermute only.
A program may use at most 128 MiB of HBM per device.

v0:
```python
import jax
import jax.numpy as jnp
from jax import lax
from jax.sharding import PartitionSpec as P


def from_behind(value, axis, by):
    devices = lax.axis_size(axis)
    pairs = [(i, i + by) for i in range(devices) if 0 <= i + by < devices]
    return lax.ppermute(value, axis, pairs)


def matmul_hi(left, right):
    return jnp.dot(left, right, precision=lax.Precision.HIGHEST, preferred_element_type=jnp.float32)


def gather_matrix(m_cols):
    return lax.all_gather(m_cols, "ctl", axis=1, tiled=True)


def earlier_sens(sens_block, reach):
    return from_behind(sens_block, "seg", reach)


def local(transition, control_map, weights):
    own_trans = transition[0]
    own_input = control_map[0]
    weight_row = weights[0]
    nseg = lax.axis_size("seg")
    nctl = lax.axis_size("ctl")
    seg_pos = lax.axis_index("seg")
    ctl_pos = lax.axis_index("ctl")
    stride = nseg // (2 * nctl)
    shard_width = own_trans.shape[1] // nctl
    blocks = [
        jnp.where(seg_pos == (2 * ctl_pos + slot_idx) * stride, own_input, 0.0)
        for slot_idx in range(2)
    ]
    sens_block = jnp.concatenate(blocks, axis=1)
    m_cols = lax.dynamic_slice_in_dim(own_trans, ctl_pos * shard_width, shard_width, 1)
    levels = (nseg - 1).bit_length()
    for level_idx in range(levels):
        reach = 1 << level_idx
        active = seg_pos >= reach
        is_last = level_idx == levels - 1
        own_whole = own_trans if level_idx == 0 else gather_matrix(m_cols)
        if is_last:
            prior_c = earlier_sens(sens_block, reach)
        else:
            prior_m, prior_c = from_behind((m_cols, sens_block), "seg", reach)
            m_cols = jnp.where(active, matmul_hi(own_whole, prior_m), m_cols)
        sens_block = jnp.where(active, matmul_hi(own_whole, prior_c) + sens_block, sens_block)
    weighted = sens_block * weight_row[:, None]
    hess_tile = lax.dot_general(
        sens_block,
        weighted,
        (((0,), (0,)), ((), ())),
        precision=lax.Precision.HIGHEST,
        preferred_element_type=jnp.float32,
    )
    summed = lax.psum(hess_tile, "seg")
    row_count = hess_tile.shape[0] // nseg
    hess_rows = lax.dynamic_slice_in_dim(summed, seg_pos * row_count, row_count, 0)
    return (sens_block[None], hess_rows[None])


def solution(mesh):
    return jax.shard_map(
        local,
        mesh=mesh,
        in_specs=(P("seg", None, None), P("seg", None, None), P("seg", None)),
        out_specs=(P("seg", None, "ctl"), P("ctl", "seg", None)),
        check_vma=False,
    )
```

profile of v0, /device:TPU:0, one launch (start us, length us, event | category | flops | bytes accessed | tf_op | source)
XLA Modules:
  0.0 375.8 jit_solution(13403189669114967752)
XLA Ops:
  7.2 1.3 constant_dynamic-slice_fusion
  8.9 5.0 %collective-permute-start = (f32[1024,256]{0,1:T(8,128)S(1)}, f32[1024,256]{0,1:T(8,128)S(1)}, u32[]{:S(2)}, u32[]{:S(2)}) collective-permute-start(f32[1024,256]{0,1:T(8,128)S(1)} %bitcast.37), channel_id=1, source_target_pairs={{0,4},{4,8},{8,12},{12,16},{16,20},{20,24},{24,28},{1,5},{5,9},{9,... | collective-permute-start | bytes 3145736 | tf_op jit(solution)/shard_map/ppermute | solution.py:10
  13.8 22.3 %collective-permute-done = f32[1024,256]{0,1:T(8,128)S(1)} collective-permute-done((f32[1024,256]{0,1:T(8,128)S(1)}, f32[1024,256]{0,1:T(8,128)S(1)}, u32[]{:S(2)}, u32[]{:S(2)}) %collective-permute-start) | collective-permute-done | bytes 1048608 | tf_op jit(solution)/shard_map/ppermute | solution.py:10
  36.2 6.9 %fusion.11 = f32[1024,256]{0,1:T(8,128)} fusion(f32[1024,256]{0,1:T(8,128)S(1)} %collective-permute-done, f32[1,1024,1024]{2,1,0:T(8,128)} %param.3, pred[]{:T(512)S(6)} %ge.11, f32[1,1024,256]{1,2,0:T(8,128)S(1)} %copy.5), kind=kOutput, calls=%fused_computation.11 | convolution fusion | flops 3221487616 | bytes 7340033 | tf_op jit(solution)/shard_map/dot_general | solution.py:14
  43.1 1.3 copy.6
  44.4 6.4 %collective-permute-start.1 = (f32[1024,256]{0,1:T(8,128)S(1)}, f32[1024,256]{0,1:T(8,128)}, u32[]{:S(2)}, u32[]{:S(2)}) collective-permute-start(f32[1024,256]{0,1:T(8,128)S(1)} %copy-done.1), channel_id=1, source_target_pairs={{0,8},{4,12},{8,16},{12,20},{16,24},{20,28},{1,9},{5,13},{9,17},{1... | collective-permute-start | bytes 3145736 | tf_op jit(solution)/shard_map/ppermute | solution.py:10
  50.8 1.6 select_bitcast_fusion.1
  52.4 1.5 pad_maximum_fusion
  53.8 3.8 %collective-permute-start.2 = (f32[1024,512]{0,1:T(8,128)}, f32[1024,512]{0,1:T(8,128)}, u32[]{:S(2)}, u32[]{:S(2)}) collective-permute-start(f32[1024,512]{0,1:T(8,128)} %pad_maximum_fusion), channel_id=1, source_target_pairs={{0,4},{4,8},{8,12},{12,16},{16,20},{20,24},{24,28},{1,5},{5,9},{9,... | collective-permute-start | bytes 6291464 | tf_op jit(solution)/shard_map/ppermute | solution.py:10
  57.6 13.7 %collective-permute-done.1 = f32[1024,256]{0,1:T(8,128)} collective-permute-done((f32[1024,256]{0,1:T(8,128)S(1)}, f32[1024,256]{0,1:T(8,128)}, u32[]{:S(2)}, u32[]{:S(2)}) %collective-permute-start.1) | collective-permute-done | bytes 1048608 | tf_op jit(solution)/shard_map/ppermute | solution.py:10
  71.3 8.6 %all-gather.3.cloned.1.call-done = f32[1024,1024]{0,1:T(8,128)} async-done(((f32[1024,256]{0,1:T(8,128)}), f32[1024,1024]{0,1:T(8,128)}) %all-gather.3.cloned.1.call-update) | async-done | bytes 4194320 | tf_op jit(solution)/shard_map/all_gather | solution.py:18
  79.9 7.3 %convolution_select_fusion = f32[1024,256]{0,1:T(8,128)} fusion(f32[1024,256]{0,1:T(8,128)S(1)} %copy-done.1, f32[1024,1024]{0,1:T(8,128)} %all-gather.3.cloned.1.call-done, f32[1024,256]{0,1:T(8,128)} %collective-permute-done.1, pred[]{:T(512)S(6)} %ge.10), kind=kOutput, calls=%fused_computation.12 | convolution fusion | flops 3221487616 | bytes 7340033 | tf_op jit(solution)/shard_map/dot_general | solution.py:14
  87.4 12.9 %collective-permute-done.2 = f32[1024,512]{0,1:T(8,128)} collective-permute-done((f32[1024,512]{0,1:T(8,128)}, f32[1024,512]{0,1:T(8,128)}, u32[]{:S(2)}, u32[]{:S(2)}) %collective-permute-start.2) | collective-permute-done | bytes 2097184 | tf_op jit(solution)/shard_map/ppermute | solution.py:10
  100.3 10.0 %add_select_fusion.2 = f32[1024,512]{0,1:T(8,128)S(1)} fusion(f32[1024,512]{0,1:T(8,128)} %collective-permute-done.2, f32[1,1024,1024]{2,1,0:T(8,128)} %param.3, pred[]{:T(512)S(6)} %ge.11, f32[1024,256]{0,1:T(8,128)S(1)} %get-tuple-element.5, f32[1024,256]{0,1:T(8,128)S(1)} %get-tuple-element.4), kind=kOutput, calls=%fused_computation.8 | convolution fusion | flops 6444023808 | bytes 10485761 | tf_op jit(solution)/shard_map/dot_general | solution.py:14
  110.3 20.6 %collective-permute-start.3 = (f32[1024,512]{0,1:T(8,128)S(1)}, f32[1024,512]{0,1:T(8,128)S(1)}, u32[]{:S(2)}, u32[]{:S(2)}) collective-permute-start(f32[1024,512]{0,1:T(8,128)S(1)} %add_select_fusion.2), channel_id=1, source_target_pairs={{0,8},{4,12},{8,16},{12,20},{16,24},{20,28},{1,9},{5,13},{9,17},{1... | collective-permute-start | bytes 6291464 | tf_op jit(solution)/shard_map/ppermute | solution.py:10
  131.0 43.0 %collective-permute-done.3 = f32[1024,512]{0,1:T(8,128)S(1)} collective-permute-done((f32[1024,512]{0,1:T(8,128)S(1)}, f32[1024,512]{0,1:T(8,128)S(1)}, u32[]{:S(2)}, u32[]{:S(2)}) %collective-permute-start.3) | collective-permute-done | bytes 2097184 | tf_op jit(solution)/shard_map/ppermute | solution.py:10
  174.0 7.0 %add_select_fusion.1 = f32[1024,512]{0,1:T(8,128)S(1)} fusion(f32[1024,512]{0,1:T(8,128)S(1)} %add_select_fusion.2, f32[1024,1024]{0,1:T(8,128)S(1)} %copy-done, f32[1024,512]{0,1:T(8,128)S(1)} %collective-permute-done.3, pred[]{:T(512)S(6)} %ge.10), kind=kOutput, calls=%fused_computation.7 | convolution fusion | flops 6443499520 | bytes 10485761 | tf_op jit(solution)/shard_map/dot_general | solution.py:14
  180.9 6.8 %collective-permute-start.4 = (f32[1024,512]{0,1:T(8,128)S(1)}, f32[1024,512]{0,1:T(8,128)}, u32[]{:S(2)}, u32[]{:S(2)}) collective-permute-start(f32[1024,512]{0,1:T(8,128)S(1)} %add_select_fusion.1), channel_id=1, source_target_pairs={{0,16},{4,20},{8,24},{12,28},{1,17},{5,21},{9,25},{13,29},{2,18},{... | collective-permute-start | bytes 6291464 | tf_op jit(solution)/shard_map/ppermute | solution.py:10
  187.7 41.0 %collective-permute-done.4 = f32[1024,512]{0,1:T(8,128)} collective-permute-done((f32[1024,512]{0,1:T(8,128)S(1)}, f32[1024,512]{0,1:T(8,128)}, u32[]{:S(2)}, u32[]{:S(2)}) %collective-permute-start.4) | collective-permute-done | bytes 2097184 | tf_op jit(solution)/shard_map/ppermute | solution.py:10
  228.7 9.8 %add_select_fusion = f32[1024,512]{0,1:T(8,128)S(1)} fusion(f32[1024,512]{0,1:T(8,128)} %copy-done.2, f32[1024,1024]{0,1:T(8,128)} %all-gather.5.cloned.1.call-done, f32[1024,512]{0,1:T(8,128)} %collective-permute-done.4, pred[]{:T(512)S(6)} %ge.9), kind=kOutput, calls=%fused_computation.6 | convolution fusion | flops 6443499520 | bytes 10485761 | tf_op jit(solution)/shard_map/dot_general | solution.py:14
  238.5 4.5 %fusion.4 = f32[512,512]{1,0:T(8,128)} fusion(f32[1024,512]{0,1:T(8,128)S(1)} %add_select_fusion, f32[1024]{0:T(1024)S(1)} %bitcast.38), kind=kOutput, calls=%fused_computation.4 | convolution fusion | flops 3221749760 | bytes 3149824 | tf_op jit(solution)/shard_map/dot_general | solution.py:54
  243.1 1.8 copy.10
  244.9 122.8 %all-reduce.2.cloned.1.call-done = f32[512,512]{1,0:T(8,128)} async-done(((f32[512,512]{1,0:T(8,128)}), f32[512,512]{1,0:T(8,128)}) %all-reduce.2.cloned.1.call-update) | async-done | bytes 1048592 | tf_op jit(solution)/shard_map/psum | solution.py:61
  367.7 1.6 dynamic-slice_bitcast_fusion
  (18 shorter events, 0.7 us)
Async XLA Ops:
  7.2 72.7 %all-gather.3.cloned.1.call-start = ((), (), s32[]{:S(2)}) async-start(), calls=%async_computation | async-start | bytes 5242880 | tf_op jit(solution)/shard_map/all_gather | solution.py:18
  8.9 27.3 %collective-permute-start = (f32[1024,256]{0,1:T(8,128)S(1)}, f32[1024,256]{0,1:T(8,128)S(1)}, u32[]{:S(2)}, u32[]{:S(2)}) collective-permute-start(f32[1024,256]{0,1:T(8,128)S(1)} %bitcast.37), channel_id=1, source_target_pairs={{0,4},{4,8},{8,12},{12,16},{16,20},{20,24},{24,28},{1,5},{5,9},{9,... | collective-permute-start | bytes 3145736 | tf_op jit(solution)/shard_map/ppermute | solution.py:10
  13.8 29.3 %copy-start.3 = (f32[1,1024,256]{2,1,0:T(8,128)S(1)}, f32[1,1024,256]{2,1,0:T(8,128)}, u32[]{:S(2)}) copy-start(f32[1,1024,256]{2,1,0:T(8,128)} %param.4) | copy-start | bytes 3145732
  43.0 1.4 copy-start.1
  43.1 185.6 %all-gather.5.cloned.1.call-start = ((), (), s32[]{:S(2)}) async-start(), calls=%async_computation.1 | async-start | bytes 5242880 | tf_op jit(solution)/shard_map/all_gather | solution.py:18
  44.4 26.9 %collective-permute-start.1 = (f32[1024,256]{0,1:T(8,128)S(1)}, f32[1024,256]{0,1:T(8,128)}, u32[]{:S(2)}, u32[]{:S(2)}) collective-permute-start(f32[1024,256]{0,1:T(8,128)S(1)} %copy-done.1), channel_id=1, source_target_pairs={{0,8},{4,12},{8,16},{12,20},{16,24},{20,28},{1,9},{5,13},{9,17},{1... | collective-permute-start | bytes 3145736 | tf_op jit(solution)/shard_map/ppermute | solution.py:10
  53.8 46.5 %collective-permute-start.2 = (f32[1024,512]{0,1:T(8,128)}, f32[1024,512]{0,1:T(8,128)}, u32[]{:S(2)}, u32[]{:S(2)}) collective-permute-start(f32[1024,512]{0,1:T(8,128)} %pad_maximum_fusion), channel_id=1, source_target_pairs={{0,4},{4,8},{8,12},{12,16},{16,20},{20,24},{24,28},{1,5},{5,9},{9,... | collective-permute-start | bytes 6291464 | tf_op jit(solution)/shard_map/ppermute | solution.py:10
  87.1 280.6 %all-reduce.2.cloned.1.call-start = ((), (), s32[]{:S(2)}) async-start(), calls=%async_computation.2 | async-start | bytes 2097152 | tf_op jit(solution)/shard_map/psum | solution.py:61
  100.3 73.7 %copy-start = (f32[1024,1024]{0,1:T(8,128)S(1)}, f32[1024,1024]{0,1:T(8,128)}, u32[]{:S(2)}) copy-start(f32[1024,1024]{0,1:T(8,128)} %all-gather.3.cloned.1.call-done) | copy-start | bytes 12582916
  110.3 63.6 %collective-permute-start.3 = (f32[1024,512]{0,1:T(8,128)S(1)}, f32[1024,512]{0,1:T(8,128)S(1)}, u32[]{:S(2)}, u32[]{:S(2)}) collective-permute-start(f32[1024,512]{0,1:T(8,128)S(1)} %add_select_fusion.2), channel_id=1, source_target_pairs={{0,8},{4,12},{8,16},{12,20},{16,24},{20,28},{1,9},{5,13},{9,17},{1... | collective-permute-start | bytes 6291464 | tf_op jit(solution)/shard_map/ppermute | solution.py:10
  180.9 47.7 %copy-start.2 = (f32[1024,512]{0,1:T(8,128)}, f32[1024,512]{0,1:T(8,128)S(1)}, u32[]{:S(2)}) copy-start(f32[1024,512]{0,1:T(8,128)S(1)} %add_select_fusion.1) | copy-start | bytes 6291460
  180.9 47.7 %collective-permute-start.4 = (f32[1024,512]{0,1:T(8,128)S(1)}, f32[1024,512]{0,1:T(8,128)}, u32[]{:S(2)}, u32[]{:S(2)}) collective-permute-start(f32[1024,512]{0,1:T(8,128)S(1)} %add_select_fusion.1), channel_id=1, source_target_pairs={{0,16},{4,20},{8,24},{12,28},{1,17},{5,21},{9,25},{13,29},{2,18},{... | collective-permute-start | bytes 6291464 | tf_op jit(solution)/shard_map/ppermute | solution.py:10
  187.7 50.8 %copy-start.4 = (f32[1,1024]{1,0:T(1,128)S(1)}, f32[1,1024]{1,0:T(1,128)}, u32[]{:S(2)}) copy-start(f32[1,1024]{1,0:T(1,128)} %param.5) | copy-start | bytes 12292
Sparse Core Ops, SparseCore 0:
  43.2 36.6 all-gather.2
  87.3 34.4 all-gather.4
  243.2 124.4 all-reduce.1
where the time goes:
time: 376 us
  waiting for transfers between devices  264 us (70%)
  matrix products  45.5 us (12%)
  starting transfers between devices  42.8 us (11%)
  between operations  13.9 us (4%)
  local copies, waits for them, and re-layouts  6.34 us (2%)
    ppermute x5, waiting for transfers between devices, from_behind(): return lax.ppermute(value, axis, pairs)  133 us
    psum x1, waiting for transfers between devices, local(): summed = lax.psum(hess_tile, 'seg')  123 us
    ppermute x5, starting transfers between devices, from_behind(): return lax.ppermute(value, axis, pairs)  42.5 us
    dot_general x5, matrix products, matmul_hi(): jnp.dot(left, right, precision=lax.Precision.HIGHEST, preferred_element_t...  40.9 us
    all_gather x2, waiting for transfers between devices, gather_matrix(): return lax.all_gather(m_cols, 'ctl', axis=1, tiled=True)  8.56 us
  transfers between devices with their start and end apart: 8, of which 7 were waited for; matrix products, arithmetic and copies ran while one was open for 8% of the time, Pallas kernels for 0%

commit v1 on v0

--- a/solution.py
+++ b/solution.py
@@ -58,7 +58,9 @@
         precision=lax.Precision.HIGHEST,
         preferred_element_type=jnp.float32,
     )
-    summed = lax.psum(hess_tile, "seg")
+    summed = hess_tile
+    for hop in (1, 2, 4):
+        summed = summed + lax.ppermute(summed, "seg", [(dev, dev ^ hop) for dev in range(8)])
     row_count = hess_tile.shape[0] // nseg
     hess_rows = lax.dynamic_slice_in_dim(summed, seg_pos * row_count, row_count, 0)
     return (sens_block[None], hess_rows[None])

time: 376 us -> 393 us (1.045)
  starting transfers between devices: 42.8 us -> 96.5 us
  waiting for transfers between devices: 264 us -> 228 us
    psum x1 -> x0, waiting for transfers between devices: 123 us -> none  [local(): summed = lax.psum(hess_tile, 'seg')]
    ppermute x0 -> x3, waiting for transfers between devices: none -> 86.6 us  [local(): lax.ppermute(summed, 'seg', [(dev, dev ^ hop) for dev in range(8)])]
    ppermute x0 -> x3, starting transfers between devices: none -> 53.7 us  [local(): lax.ppermute(summed, 'seg', [(dev, dev ^ hop) for dev in range(8)])]
  transfers between devices with their start and end apart: 8 -> 10, of which waited for: 7 -> 9; matrix products, arithmetic and copies ran while one was open for 8% -> 8% of each run, Pallas kernels for 0% -> 0%
where the time goes in v1:
time: 393 us
  waiting for transfers between devices  228 us (58%)
  starting transfers between devices  96.5 us (25%)
  matrix products  44.5 us (11%)
  between operations  14.2 us (4%)
  other arithmetic  5.02 us (1%)
  local copies, waits for them, and re-layouts  4.76 us (1%)
    ppermute x5, waiting for transfers between devices, from_behind(): return lax.ppermute(value, axis, pairs)  133 us
    ppermute x3, waiting for transfers between devices, local(): lax.ppermute(summed, 'seg', [(dev, dev ^ hop) for dev in range(8)])  86.6 us
    ppermute x3, starting transfers between devices, local(): lax.ppermute(summed, 'seg', [(dev, dev ^ hop) for dev in range(8)])  53.7 us
    ppermute x5, starting transfers between devices, from_behind(): return lax.ppermute(value, axis, pairs)  42.7 us
    dot_general x5, matrix products, matmul_hi(): jnp.dot(left, right, precision=lax.Precision.HIGHEST, preferred_element_t...  40.9 us
    all_gather x2, waiting for transfers between devices, gather_matrix(): return lax.all_gather(m_cols, 'ctl', axis=1, tiled=True)  8.56 us
  transfers between devices with their start and end apart: 10, of which 9 were waited for; matrix products, arithmetic and copies ran while one was open for 8% of the time, Pallas kernels for 0%

profile of v1, /device:TPU:0, one launch (start us, length us, event | category | flops | bytes accessed | tf_op | source)
XLA Modules:
  0.0 393.0 jit_solution(2678284901564741933)
XLA Ops:
  8.9 5.0 %collective-permute-start = (f32[1024,256]{0,1:T(8,128)S(1)}, f32[1024,256]{0,1:T(8,128)S(1)}, u32[]{:S(2)}, u32[]{:S(2)}) collective-permute-start(f32[1024,256]{0,1:T(8,128)S(1)} %bitcast.37), channel_id=1, source_target_pairs={{0,4},{4,8},{8,12},{12,16},{16,20},{20,24},{24,28},{1,5},{5,9},{9,... | collective-permute-start | bytes 3145736 | tf_op jit(solution)/shard_map/ppermute | solution.py:10
  13.8 22.3 %collective-permute-done = f32[1024,256]{0,1:T(8,128)S(1)} collective-permute-done((f32[1024,256]{0,1:T(8,128)S(1)}, f32[1024,256]{0,1:T(8,128)S(1)}, u32[]{:S(2)}, u32[]{:S(2)}) %collective-permute-start) | collective-permute-done | bytes 1048608 | tf_op jit(solution)/shard_map/ppermute | solution.py:10
  36.2 6.9 %fusion.11 = f32[1024,256]{0,1:T(8,128)} fusion(f32[1024,256]{0,1:T(8,128)S(1)} %collective-permute-done, f32[1,1024,1024]{2,1,0:T(8,128)} %param.3, pred[]{:T(512)S(6)} %ge.11, f32[1,1024,256]{1,2,0:T(8,128)S(1)} %copy.5), kind=kOutput, calls=%fused_computation.11 | convolution fusion | flops 3221487616 | bytes 7340033 | tf_op jit(solution)/shard_map/dot_general | solution.py:14
  44.4 6.3 %collective-permute-start.1 = (f32[1024,256]{0,1:T(8,128)S(1)}, f32[1024,256]{0,1:T(8,128)}, u32[]{:S(2)}, u32[]{:S(2)}) collective-permute-start(f32[1024,256]{0,1:T(8,128)S(1)} %copy-done.1), channel_id=1, source_target_pairs={{0,8},{4,12},{8,16},{12,20},{16,24},{20,28},{1,9},{5,13},{9,17},{1... | collective-permute-start | bytes 3145736 | tf_op jit(solution)/shard_map/ppermute | solution.py:10
  53.8 3.8 collective-permute-start.2
  57.6 13.7 %collective-permute-done.1 = f32[1024,256]{0,1:T(8,128)} collective-permute-done((f32[1024,256]{0,1:T(8,128)S(1)}, f32[1024,256]{0,1:T(8,128)}, u32[]{:S(2)}, u32[]{:S(2)}) %collective-permute-start.1) | collective-permute-done | bytes 1048608 | tf_op jit(solution)/shard_map/ppermute | solution.py:10
  71.3 8.6 %all-gather.3.cloned.1.call-done = f32[1024,1024]{0,1:T(8,128)} async-done(((f32[1024,256]{0,1:T(8,128)}), f32[1024,1024]{0,1:T(8,128)}) %all-gather.3.cloned.1.call-update) | async-done | bytes 4194320 | tf_op jit(solution)/shard_map/all_gather | solution.py:18
  79.9 7.2 %convolution_select_fusion = f32[1024,256]{0,1:T(8,128)} fusion(f32[1024,256]{0,1:T(8,128)S(1)} %copy-done.1, f32[1024,1024]{0,1:T(8,128)} %all-gather.3.cloned.1.call-done, f32[1024,256]{0,1:T(8,128)} %collective-permute-done.1, pred[]{:T(512)S(6)} %ge.10), kind=kOutput, calls=%fused_computation.12 | convolution fusion | flops 3221487616 | bytes 7340033 | tf_op jit(solution)/shard_map/dot_general | solution.py:14
  87.1 13.2 %collective-permute-done.2 = f32[1024,512]{0,1:T(8,128)} collective-permute-done((f32[1024,512]{0,1:T(8,128)}, f32[1024,512]{0,1:T(8,128)}, u32[]{:S(2)}, u32[]{:S(2)}) %collective-permute-start.2) | collective-permute-done | bytes 2097184 | tf_op jit(solution)/shard_map/ppermute | solution.py:10
  100.3 10.0 %add_select_fusion.2 = f32[1024,512]{0,1:T(8,128)S(1)} fusion(f32[1024,512]{0,1:T(8,128)} %collective-permute-done.2, f32[1,1024,1024]{2,1,0:T(8,128)} %param.3, pred[]{:T(512)S(6)} %ge.11, f32[1024,256]{0,1:T(8,128)S(1)} %get-tuple-element.5, f32[1024,256]{0,1:T(8,128)S(1)} %get-tuple-element.4), kind=kOutput, calls=%fused_computation.8 | convolution fusion | flops 6444023808 | bytes 10485761 | tf_op jit(solution)/shard_map/dot_general | solution.py:14
  110.3 20.9 %collective-permute-start.3 = (f32[1024,512]{0,1:T(8,128)S(1)}, f32[1024,512]{0,1:T(8,128)S(1)}, u32[]{:S(2)}, u32[]{:S(2)}) collective-permute-start(f32[1024,512]{0,1:T(8,128)S(1)} %add_select_fusion.2), channel_id=1, source_target_pairs={{0,8},{4,12},{8,16},{12,20},{16,24},{20,28},{1,9},{5,13},{9,17},{1... | collective-permute-start | bytes 6291464 | tf_op jit(solution)/shard_map/ppermute | solution.py:10
  131.2 42.8 %collective-permute-done.3 = f32[1024,512]{0,1:T(8,128)S(1)} collective-permute-done((f32[1024,512]{0,1:T(8,128)S(1)}, f32[1024,512]{0,1:T(8,128)S(1)}, u32[]{:S(2)}, u32[]{:S(2)}) %collective-permute-start.3) | collective-permute-done | bytes 2097184 | tf_op jit(solution)/shard_map/ppermute | solution.py:10
  174.0 7.0 %add_select_fusion.1 = f32[1024,512]{0,1:T(8,128)S(1)} fusion(f32[1024,512]{0,1:T(8,128)S(1)} %add_select_fusion.2, f32[1024,1024]{0,1:T(8,128)S(1)} %copy-done, f32[1024,512]{0,1:T(8,128)S(1)} %collective-permute-done.3, pred[]{:T(512)S(6)} %ge.10), kind=kOutput, calls=%fused_computation.7 | convolution fusion | flops 6443499520 | bytes 10485761 | tf_op jit(solution)/shard_map/dot_general | solution.py:14
  180.9 6.7 %collective-permute-start.4 = (f32[1024,512]{0,1:T(8,128)S(1)}, f32[1024,512]{0,1:T(8,128)}, u32[]{:S(2)}, u32[]{:S(2)}) collective-permute-start(f32[1024,512]{0,1:T(8,128)S(1)} %add_select_fusion.1), channel_id=1, source_target_pairs={{0,16},{4,20},{8,24},{12,28},{1,17},{5,21},{9,25},{13,29},{2,18},{... | collective-permute-start | bytes 6291464 | tf_op jit(solution)/shard_map/ppermute | solution.py:10
  187.7 41.0 %collective-permute-done.4 = f32[1024,512]{0,1:T(8,128)} collective-permute-done((f32[1024,512]{0,1:T(8,128)S(1)}, f32[1024,512]{0,1:T(8,128)}, u32[]{:S(2)}, u32[]{:S(2)}) %collective-permute-start.4) | collective-permute-done | bytes 2097184 | tf_op jit(solution)/shard_map/ppermute | solution.py:10
  228.7 9.8 %add_select_fusion = f32[1024,512]{0,1:T(8,128)S(1)} fusion(f32[1024,512]{0,1:T(8,128)} %copy-done.2, f32[1024,1024]{0,1:T(8,128)} %all-gather.5.cloned.1.call-done, f32[1024,512]{0,1:T(8,128)} %collective-permute-done.4, pred[]{:T(512)S(6)} %ge.9), kind=kOutput, calls=%fused_computation.6 | convolution fusion | flops 6443499520 | bytes 10485761 | tf_op jit(solution)/shard_map/dot_general | solution.py:14
  238.5 3.5 fusion.4
  242.1 21.5 %collective-permute-done.5 = f32[512,512]{1,0:T(8,128)S(1)} collective-permute-done((f32[512,512]{1,0:T(8,128)S(1)}, f32[512,512]{1,0:T(8,128)S(1)}, u32[]{:S(2)}, u32[]{:S(2)}) %collective-permute-start.5) | collective-permute-done | bytes 1048608 | tf_op jit(solution)/shard_map/ppermute | solution.py:63
  263.8 50.0 %collective-permute-start.6 = (f32[512,512]{1,0:T(8,128)S(1)}, f32[512,512]{1,0:T(8,128)S(1)}, u32[]{:S(2)}, u32[]{:S(2)}) collective-permute-start(f32[512,512]{1,0:T(8,128)S(1)} %add.32), channel_id=1, source_target_pairs={{0,8},{4,12},{8,0},{12,4},{16,24},{20,28},{24,16},{28,20},{1,9},{5... | collective-permute-start | bytes 3145736 | tf_op jit(solution)/shard_map/ppermute | solution.py:63
  313.8 22.5 %collective-permute-done.6 = f32[512,512]{1,0:T(8,128)S(1)} collective-permute-done((f32[512,512]{1,0:T(8,128)S(1)}, f32[512,512]{1,0:T(8,128)S(1)}, u32[]{:S(2)}, u32[]{:S(2)}) %collective-permute-start.6) | collective-permute-done | bytes 1048608 | tf_op jit(solution)/shard_map/ppermute | solution.py:63
  336.5 3.6 collective-permute-start.7
  340.1 1.8 copy.10
  341.9 42.7 %collective-permute-done.7 = f32[512,512]{1,0:T(8,128)} collective-permute-done((f32[512,512]{1,0:T(8,128)S(1)}, f32[512,512]{1,0:T(8,128)}, u32[]{:S(2)}, u32[]{:S(2)}) %collective-permute-start.7) | collective-permute-done | bytes 1048608 | tf_op jit(solution)/shard_map/ppermute | solution.py:63
  384.6 1.6 fusion.15
  (23 shorter events, 6.6 us)
Async XLA Ops:
  7.2 72.7 %all-gather.3.cloned.1.call-start = ((), (), s32[]{:S(2)}) async-start(), calls=%async_computation | async-start | bytes 5242880 | tf_op jit(solution)/shard_map/all_gather | solution.py:18
  8.9 27.3 %collective-permute-start = (f32[1024,256]{0,1:T(8,128)S(1)}, f32[1024,256]{0,1:T(8,128)S(1)}, u32[]{:S(2)}, u32[]{:S(2)}) collective-permute-start(f32[1024,256]{0,1:T(8,128)S(1)} %bitcast.37), channel_id=1, source_target_pairs={{0,4},{4,8},{8,12},{12,16},{16,20},{20,24},{24,28},{1,5},{5,9},{9,... | collective-permute-start | bytes 3145736 | tf_op jit(solution)/shard_map/ppermute | solution.py:10
  13.8 29.3 %copy-start.3 = (f32[1,1024,256]{2,1,0:T(8,128)S(1)}, f32[1,1024,256]{2,1,0:T(8,128)}, u32[]{:S(2)}) copy-start(f32[1,1024,256]{2,1,0:T(8,128)} %param.4) | copy-start | bytes 3145732
  43.0 1.4 copy-start.1
  43.0 185.6 %all-gather.5.cloned.1.call-start = ((), (), s32[]{:S(2)}) async-start(), calls=%async_computation.1 | async-start | bytes 5242880 | tf_op jit(solution)/shard_map/all_gather | solution.py:18
  44.4 26.9 %collective-permute-start.1 = (f32[1024,256]{0,1:T(8,128)S(1)}, f32[1024,256]{0,1:T(8,128)}, u32[]{:S(2)}, u32[]{:S(2)}) collective-permute-start(f32[1024,256]{0,1:T(8,128)S(1)} %copy-done.1), channel_id=1, source_target_pairs={{0,8},{4,12},{8,16},{12,20},{16,24},{20,28},{1,9},{5,13},{9,17},{1... | collective-permute-start | bytes 3145736 | tf_op jit(solution)/shard_map/ppermute | solution.py:10
  53.8 46.5 %collective-permute-start.2 = (f32[1024,512]{0,1:T(8,128)}, f32[1024,512]{0,1:T(8,128)}, u32[]{:S(2)}, u32[]{:S(2)}) collective-permute-start(f32[1024,512]{0,1:T(8,128)} %pad_maximum_fusion), channel_id=1, source_target_pairs={{0,4},{4,8},{8,12},{12,16},{16,20},{20,24},{24,28},{1,5},{5,9},{9,... | collective-permute-start | bytes 6291464 | tf_op jit(solution)/shard_map/ppermute | solution.py:10
  100.3 73.7 %copy-start = (f32[1024,1024]{0,1:T(8,128)S(1)}, f32[1024,1024]{0,1:T(8,128)}, u32[]{:S(2)}) copy-start(f32[1024,1024]{0,1:T(8,128)} %all-gather.3.cloned.1.call-done) | copy-start | bytes 12582916
  110.3 63.6 %collective-permute-start.3 = (f32[1024,512]{0,1:T(8,128)S(1)}, f32[1024,512]{0,1:T(8,128)S(1)}, u32[]{:S(2)}, u32[]{:S(2)}) collective-permute-start(f32[1024,512]{0,1:T(8,128)S(1)} %add_select_fusion.2), channel_id=1, source_target_pairs={{0,8},{4,12},{8,16},{12,20},{16,24},{20,28},{1,9},{5,13},{9,17},{1... | collective-permute-start | bytes 6291464 | tf_op jit(solution)/shard_map/ppermute | solution.py:10
  180.9 47.7 %copy-start.2 = (f32[1024,512]{0,1:T(8,128)}, f32[1024,512]{0,1:T(8,128)S(1)}, u32[]{:S(2)}) copy-start(f32[1024,512]{0,1:T(8,128)S(1)} %add_select_fusion.1) | copy-start | bytes 6291460
  180.9 47.7 %collective-permute-start.4 = (f32[1024,512]{0,1:T(8,128)S(1)}, f32[1024,512]{0,1:T(8,128)}, u32[]{:S(2)}, u32[]{:S(2)}) collective-permute-start(f32[1024,512]{0,1:T(8,128)S(1)} %add_select_fusion.1), channel_id=1, source_target_pairs={{0,16},{4,20},{8,24},{12,28},{1,17},{5,21},{9,25},{13,29},{2,18},{... | collective-permute-start | bytes 6291464 | tf_op jit(solution)/shard_map/ppermute | solution.py:10
  187.7 50.8 %copy-start.4 = (f32[1,1024]{1,0:T(1,128)S(1)}, f32[1,1024]{1,0:T(1,128)}, u32[]{:S(2)}) copy-start(f32[1,1024]{1,0:T(1,128)} %param.5) | copy-start | bytes 12292
  242.1 21.5 %collective-permute-start.5 = (f32[512,512]{1,0:T(8,128)S(1)}, f32[512,512]{1,0:T(8,128)S(1)}, u32[]{:S(2)}, u32[]{:S(2)}) collective-permute-start(f32[512,512]{1,0:T(8,128)S(1)} %fusion.4), channel_id=1, source_target_pairs={{0,4},{4,0},{8,12},{12,8},{16,20},{20,16},{24,28},{28,24},{1,5},{5... | collective-permute-start | bytes 3145736 | tf_op jit(solution)/shard_map/ppermute | solution.py:63
  263.8 72.5 %collective-permute-start.6 = (f32[512,512]{1,0:T(8,128)S(1)}, f32[512,512]{1,0:T(8,128)S(1)}, u32[]{:S(2)}, u32[]{:S(2)}) collective-permute-start(f32[512,512]{1,0:T(8,128)S(1)} %add.32), channel_id=1, source_target_pairs={{0,8},{4,12},{8,0},{12,4},{16,24},{20,28},{24,16},{28,20},{1,9},{5... | collective-permute-start | bytes 3145736 | tf_op jit(solution)/shard_map/ppermute | solution.py:63
  336.5 48.0 %collective-permute-start.7 = (f32[512,512]{1,0:T(8,128)S(1)}, f32[512,512]{1,0:T(8,128)}, u32[]{:S(2)}, u32[]{:S(2)}) collective-permute-start(f32[512,512]{1,0:T(8,128)S(1)} %add.33), channel_id=1, source_target_pairs={{0,16},{4,20},{8,24},{12,28},{16,0},{20,4},{24,8},{28,12},{1,17},{... | collective-permute-start | bytes 3145736 | tf_op jit(solution)/shard_map/ppermute | solution.py:63
Sparse Core Ops, SparseCore 0:
  43.2 36.6 all-gather.2
  87.2 34.4 all-gather.4
